TPU v7x, 256 devices: a whole 4x4x8 slice. The times are simulated.
256 devices in a mesh: tm: 32 (over z, x_hi, core), chan: 8 (over x_lo, y).
Axes of the slice: x: 4 (x_hi: 2, x_lo: 2; x = x_hi * 2 + x_lo), y: 4, z: 8, core: 2. Of those that a mesh axis runs over, the one named last changes fastest.
Arguments:
- raw_traces: bfloat16 [5120, 131072], P('chan', 'tm'), may hold values from -120 to 120
- fir_taps: bfloat16 [128], replicated, may hold values from -0.5 to 0.5
- sources: int32 [512], replicated, may hold values from 0 to 5119, as said below
- dead_flags: int32 [5120], P('chan'), may hold values 0 or 1
Outputs:
- correlations: float32 [512, 8, 5120], P('tm', None, 'chan')
Inputs may be any that keep to these rules, and one draw needn't show every extreme that they name: `sources`: 512 distinct channel indices; no group of 640 channels that share c // 640 holds more than 128 of them, and one group holds exactly 128.
All inputs are finite; a program needn't handle non-finite values. No bound on the sum of `dead_flags` on one device may be relied on, other than what follows from the above.
Results may differ from a plain program's by a relative error of at most 0.013.
Values may be sent and summed in bfloat16 or wider, within the bound.
A program may use at most 64 MiB of HBM per device.

v0:
```python
import math

import jax
import jax.numpy as jnp
from jax import lax
from jax.sharding import PartitionSpec as P

VS = 512
TD = 256
NWIN = 4
NLAG = 8
HW = 32
TAPS = 128
DECIM = 4


def from_behind(value, axis, steps):
    count = lax.axis_size(axis)
    initial, last = (max(0, -steps), min(count, count - steps))
    return lax.ppermute(value, axis, [(source, source + steps) for source in range(initial, last)])


def fir_rows(fir_taps, out_block):
    width = TAPS + DECIM * out_block
    padded_taps = jnp.concatenate(
        [
            jnp.zeros((1,), jnp.bfloat16),
            fir_taps,
            jnp.zeros((width + DECIM - TAPS - 1,), jnp.bfloat16),
        ]
    )
    return jnp.tile(padded_taps, out_block)[: out_block * width].reshape(out_block, width)


def dft_table():
    time_index = jnp.arange(TD)[:, None]
    freq_index = jnp.arange(TD // 2)[None, :]
    phase = time_index * freq_index % TD
    angles = 2.0 * math.pi / TD * phase.astype(jnp.float32)
    return jnp.concatenate([jnp.cos(angles), -jnp.sin(angles)], axis=1).astype(jnp.bfloat16)


def lag_tables():
    lag_shift = jnp.arange(NLAG) - NLAG // 2
    freq_index = jnp.arange(TD // 2)
    phase = lag_shift[:, None] * freq_index[None, :] % TD
    angles = 2.0 * math.pi / TD * phase.astype(jnp.float32)
    return (jnp.cos(angles), jnp.sin(angles))


def band_matrix():
    bin_index = jnp.arange(TD // 2)
    return (jnp.abs(bin_index[:, None] - bin_index[None, :]) <= HW).astype(jnp.float32)


def whiten(spectrum, alive):
    half_bins = TD // 2
    real_part = spectrum[..., :half_bins]
    imag_part = spectrum[..., half_bins:]
    amplitude = jnp.sqrt(real_part * real_part + imag_part * imag_part)
    mean_level = jnp.einsum(
        "cwf,fg->cwg", amplitude, band_matrix(), precision=lax.Precision.HIGHEST
    ) / (2 * HW + 1)
    factor = alive / (mean_level + 1e-06)
    return (spectrum * jnp.concatenate([factor, factor], axis=-1)).astype(jnp.bfloat16)


def rotate(source, gain_scale):
    half_bins = TD // 2
    real_src = source[..., :half_bins].astype(jnp.float32)[:, None]
    imag_src = source[..., half_bins:].astype(jnp.float32)[:, None]
    cos_lag, sin_lag = lag_tables()
    cos_lag = cos_lag[None, :, None, :]
    sin_lag = sin_lag[None, :, None, :]
    real_out = (real_src * cos_lag + imag_src * sin_lag) * gain_scale
    imag_out = (imag_src * cos_lag - real_src * sin_lag) * gain_scale
    return jnp.concatenate([real_out, imag_out], axis=-1).astype(jnp.bfloat16)


def local(raw_traces, fir_taps, sources, dead_flags):
    chan_rows = raw_traces.shape[0]
    time_parts = lax.axis_size("tm")
    group_index = lax.axis_index("chan")
    history = from_behind(raw_traces[:, raw_traces.shape[1] - TAPS :], "tm", 1)
    out_block = min(128, raw_traces.shape[1] // DECIM)
    sample_block = DECIM * out_block
    grouped = raw_traces.reshape(chan_rows, -1, sample_block)
    before = jnp.concatenate([history[:, None, :], grouped[:, :-1, sample_block - TAPS :]], axis=1)
    window = jnp.concatenate([before, grouped], axis=2).reshape(-1, TAPS + sample_block)
    dec = jnp.dot(window, fir_rows(fir_taps, out_block).T, preferred_element_type=jnp.float32)
    dec = dec.astype(jnp.bfloat16).reshape(chan_rows, -1)
    spectrum = jnp.dot(
        dec.reshape(-1, TD), dft_table(), preferred_element_type=jnp.float32
    ).reshape(chan_rows, -1, TD)
    alive = (1 - dead_flags).astype(jnp.float32)[:, None, None]
    whitened = whiten(spectrum, alive)
    white_flat = whitened.reshape(chan_rows, -1)
    first_chan = group_index * chan_rows
    chan_match = (sources[:, None] - first_chan == jnp.arange(chan_rows)[None, :]).astype(
        jnp.bfloat16
    )
    picked = jnp.dot(chan_match, white_flat, preferred_element_type=jnp.float32)
    source = lax.psum(picked.astype(jnp.bfloat16), "chan")
    gain_scale = 1.0 / math.sqrt(time_parts * NWIN * TD)
    lagged = rotate(source.reshape(VS, -1, TD), gain_scale).reshape(VS * NLAG, -1)
    stacked = lax.psum_scatter(
        lax.dot_general(
            lagged, white_flat, (((1,), (1,)), ((), ())), preferred_element_type=jnp.float32
        ).astype(jnp.bfloat16),
        "tm",
        scatter_dimension=0,
        tiled=True,
    ).astype(jnp.float32)
    return stacked.reshape(-1, NLAG, chan_rows)


def solution(mesh):
    return jax.shard_map(
        local,
        mesh=mesh,
        in_specs=(P("chan", "tm"), P(), P(), P("chan")),
        out_specs=P("tm", None, "chan"),
        check_vma=False,
    )
```

profile of v0, /device:TPU:2, one launch (start us, length us, event | category | flops | bytes accessed | tf_op | source)
XLA Modules:
  0.0 298.6 jit_solution(4898758762100365778)
XLA Ops:
  6.5 0.9 slice.21
  7.5 1.7 collective-permute-start
  9.2 0.7 subtract_convert_fusion
  9.9 0.7 broadcast_subtract_fusion
  10.6 0.7 pad_maximum_fusion
  11.3 8.9 %concatenate.27 = bf16[5120,512]{1,0:T(8,128)(2,1)} reshape(bf16[640,4096]{1,0:T(8,128)(2,1)} %param.4) | data formatting | bytes 10485760 | tf_op jit(solution)/shard_map/concatenate | solution.py:89
  20.3 0.4 tile.10
  20.7 0.1 reshape.94
  20.8 6.2 %copy.12 = bf16[80,8,8,512]{3,2,1,0:T(8,128)(2,1)S(1)} copy(bf16[80,8,8,512]{3,1,2,0:T(8,128)(2,1)} %bitcast.23) | data formatting | bytes 10485760
  27.0 0.2 slice.28
  27.2 0.5 negate_convert_fusion
  27.7 0.3 copy.8
  28.0 0.7 maximum_bitcast_fusion.1
  28.7 2.1 fusion.4
  30.8 0.9 dot_general.18
  31.7 0.5 fusion.13
  32.2 1.4 fusion.9
  33.6 0.3 fusion.7
  34.0 1.0 convolution_convert_fusion.1
  35.0 1.6 reshape.96
  36.5 0.0 all-reduce.2.cloned.1.call-update
  36.6 0.2 reduce-scatter.2.cloned.1.call-start
  36.8 0.1 fusion.34
  36.9 85.8 %all-reduce.2.cloned.1.call-done = bf16[512,4,256]{2,1,0:T(4,128)(2,1)} async-done(((bf16[512,4,256]{2,1,0:T(4,128)(2,1)}), bf16[512,4,256]{2,1,0:T(4,128)(2,1)}) %all-reduce.2.cloned.1.call-update) | async-done | bytes 1048592 | tf_op jit(solution)/shard_map/psum | solution.py:103
  122.7 1.3 slice_convert_fusion.1
  124.0 5.5 %multiply_convert_fusion.1 = (bf16[512,8,4,128]{3,2,1,0:T(4,128)(2,1)S(1)}, bf16[512,8,4,128]{3,2,1,0:T(4,128)(2,1)S(1)}) fusion(f32[8,128]{1,0:T(8,128)S(1)} %get-tuple-element.10, f32[512,4,128]{2,1,0:T(4,128)S(1)} %get-tuple-element.8, f32[8,128]{1,0:T(8,128)S(1)} %get-tuple-element.9, f32[512,4,128]{2,1,0:T(4,128)S(1)} %get-tuple-element.7), kind=kLoop, calls=%fused_computation.2 | loop fusion | flops 20971520 | bytes 10493952 | tf_op jit(solution)/shard_map/convert.1
  129.5 6.6 %maximum_bitcast_fusion = bf16[512,8,4,256]{3,2,1,0:T(4,128)(2,1)} fusion(bf16[512,8,4,128]{3,2,1,0:T(4,128)(2,1)S(1)} %get-tuple-element.6, bf16[512,8,4,128]{3,2,1,0:T(4,128)(2,1)S(1)} %get-tuple-element.5), kind=kLoop, calls=%fused_computation | loop fusion | flops 16777216 | bytes 16777216
  136.1 9.4 %copy.13 = bf16[512,8,4,256]{3,1,2,0:T(8,128)(2,1)} copy(bf16[512,8,4,256]{3,2,1,0:T(4,128)(2,1)} %maximum_bitcast_fusion) | data formatting | bytes 16777216
  145.5 11.5 %convolution_convert_fusion = bf16[4096,640]{1,0:T(8,128)(2,1)} fusion(bf16[4096,1024]{1,0:T(8,128)(2,1)} %bitcast.24, bf16[640,1024]{0,1:T(8,128)(2,1)S(1)} %bitcast.29), kind=kOutput, calls=%fused_computation.7 | convolution fusion | flops 5371330560 | bytes 14942208 | tf_op jit(solution)/shard_map/dot_general | solution.py:107
  157.0 0.0 reduce-scatter.2.cloned.1.call-update
  157.0 133.1 %reduce-scatter.2.cloned.1.call-done = bf16[128,640]{1,0:T(8,128)(2,1)} async-done(((bf16[4096,640]{1,0:T(8,128)(2,1)}), bf16[128,640]{1,0:T(8,128)(2,1)}) %reduce-scatter.2.cloned.1.call-update) | async-done | bytes 163856 | tf_op jit(solution)/shard_map/reduce_scatter | solution.py:106
  290.1 1.7 bitcast_convert_fusion
  (11 shorter events, 0.1 us)
Async XLA Ops:
  6.5 116.2 %all-reduce.2.cloned.1.call-start = ((), (), s32[]{:S(2)}) async-start(), calls=%async_computation.1 | async-start | bytes 2097152 | tf_op jit(solution)/shard_map/psum | solution.py:103
  7.5 20.2 %collective-permute-start = (bf16[640,128]{1,0:T(8,128)(2,1)S(1)}, bf16[640,128]{1,0:T(8,128)(2,1)S(1)}, u32[]{:S(2)}, u32[]{:S(2)}) collective-permute-start(bf16[640,128]{1,0:T(8,128)(2,1)S(1)} %slice.21), channel_id=1, source_target_pairs={{0,8},{8,16},{16,24},{24,32},{32,40},{40,48},{48,56},{56,64},{64,7... | collective-permute-start | bytes 491528 | tf_op jit(solution)/shard_map/ppermute | solution.py:20
  20.8 7.9 %slice-start = ((s8[5242880]{0:T(1024)(128)(4,1)}), s8[4194304]{0:T(1024)(128)(4,1)S(1)}, s32[]{:S(2)}) async-start(s8[5242880]{0:T(1024)(128)(4,1)} %bitcast.26), calls=%async_computation.3 | async-start | bytes 8388608
  20.8 7.9 %slice-start.1 = ((s8[5242880]{0:T(1024)(128)(4,1)}), s8[1048576]{0:T(1024)(128)(4,1)S(1)}, s32[]{:S(2)}) async-start(s8[5242880]{0:T(1024)(128)(4,1)} %bitcast.26), calls=%async_computation.4 | async-start | bytes 2097152
  36.6 253.5 %reduce-scatter.2.cloned.1.call-start = ((), (), s32[]{:S(2)}) async-start(), calls=%async_computation.2 | async-start | bytes 5406720 | tf_op jit(solution)/shard_map/reduce_scatter | solution.py:106
Sparse Core Ops, SparseCore 0:
  36.7 85.9 all-reduce.1
  157.1 132.9 reduce-scatter.1
where the time goes:
time: 300 us; the launch traced here: 299 us
  waiting for transfers between devices  219 us (73%)
  local copies, waits for them, and re-layouts  28.8 us (10%)
  other arithmetic  18.9 us (6%)
  matrix products  16.5 us (6%)
  between operations  13.6 us (5%)
    reduce_scatter x1, waiting for transfers between devices, local(): lax.psum_scatter(lax.dot_general(lagged, white_flat, (((1,), (1,)), ((),...  133 us
    psum x1, waiting for transfers between devices, local(): source = lax.psum(picked.astype(jnp.bfloat16), 'chan')  85.8 us
    unnamed x6, local copies, waits for them, and re-layouts  15.5 us
    dot_general x1, matrix products, local(): lax.dot_general(lagged, white_flat, (((1,), (1,)), ((), ())), preferred_e...  11.5 us
    concatenate x1, local copies, waits for them, and re-layouts, local(): jnp.concatenate([before, grouped], axis=2).reshape(-1, TAPS + sample_block)  8.92 us
    unnamed x2, other arithmetic  6.63 us
    another operation x2, other arithmetic  6.01 us
  transfers between devices with their start and end apart: 3, of which 2 were waited for; matrix products, arithmetic and copies ran while one was open for 6% of the time, Pallas kernels for 0%

commit v1 on v0

v1 whole, which is shorter than its diff:
```python
import functools
import math

import jax
import jax.numpy as jnp
import numpy as np
from jax import lax
from jax.experimental import pallas as pl
from jax.experimental.pallas import tpu as pltpu
from jax.sharding import PartitionSpec as P

VS = 512
TD = 256
NWIN = 4
NLAG = 8
HW = 32
TAPS = 128
DECIM = 4
HALF = TD // 2
MESH = pl.DeviceIdType.MESH
F32 = jnp.float32
BF16 = jnp.bfloat16
NT = (((1,), (1,)), ((), ()))

ZN = 8
GN = 8
SUBS = 2
LEAD_AG = 2
LEAD_RS = 4


def fir_rows(fir_taps, out_block):
    width = TAPS + DECIM * out_block
    padded_taps = jnp.concatenate(
        [jnp.zeros((1,), BF16), fir_taps, jnp.zeros((width + DECIM - TAPS - 1,), BF16)]
    )
    return jnp.tile(padded_taps, out_block)[: out_block * width].reshape(out_block, width)


def dft_table():
    phase = np.arange(TD)[:, None] * np.arange(HALF)[None, :] % TD
    angles = np.float32(2.0 * math.pi / TD) * phase.astype(np.float32)
    return jnp.asarray(np.concatenate([np.cos(angles), -np.sin(angles)], axis=1), dtype=BF16)


def lag_tables(gain):
    phase = np.arange(NLAG)[:, None] * np.arange(HALF)[None, :] % TD
    angles = np.float32(2.0 * math.pi / TD) * phase.astype(np.float32)
    both = np.concatenate([np.cos(angles), np.sin(angles)], axis=1)
    return jnp.asarray((both * np.float32(gain)).astype(np.float32))


def band_matrix():
    bins = np.arange(HALF)
    return jnp.asarray(np.abs(bins[:, None] - bins[None, :]) <= HW, dtype=BF16)


def kernel(
    raw_ref, fir_ref, table_ref, band_ref, lag_ref, src_ref, dead_ref, out_ref,
    raw, w2, picked, landed, gath, lagged, part, going, coming, kept, xgoing, xcoming,
    raw_sem, hist_sem, sib_ss, sib_rs, rs_ss, rs_rs, ag_ss, ag_rs, ring_ss, ring_rs, x_ss, x_rs,
):
    rows = raw_ref.shape[0]
    samples = raw_ref.shape[1]
    win_raw = TD * DECIM
    seg_cols = NWIN * TD
    per_stage = VS // (2 * ZN)
    per_dest = per_stage // 2
    sub_rows = rows // SUBS
    t, g = lax.axis_index("tm"), lax.axis_index("chan")
    tn = lax.axis_size("tm")
    z, xh, c = t // 4, (t // 2) % 2, t % 2
    sibling = (t + 1 - 2 * c, g)
    above = (((z + 1) % ZN) * 4 + xh * 2 + c, g)
    below = (((z + ZN - 1) % ZN) * 4 + xh * 2 + c, g)
    across = (z * 4 + (1 - xh) * 2 + c, g)
    later = ((t + 1) % tn, g)
    earlier = ((t + tn - 1) % tn, g)

    def member(r):
        return (t, (g + r) % GN)

    raw_copies = []
    for w in range(NWIN):
        raw_copies.append(
            pltpu.make_async_copy(
                raw_ref.at[:, pl.ds(w * win_raw, win_raw)],
                raw.at[:, pl.ds(TAPS + w * win_raw, win_raw)],
                raw_sem.at[w],
            )
        )
    for w in reversed(range(NWIN)):
        raw_copies[w].start()

    barrier = pltpu.get_barrier_semaphore()
    peers = [sibling, above, below, across, later, earlier] + [member(r) for r in range(1, GN)]
    for peer in peers:
        pl.semaphore_signal(barrier, inc=1, device_id=peer, device_id_type=MESH)
    pl.semaphore_wait(barrier, len(peers))

    history = pltpu.make_async_remote_copy(
        src_ref=raw_ref.at[:, pl.ds(samples - TAPS, TAPS)],
        dst_ref=raw.at[:, pl.ds(0, TAPS)],
        send_sem=hist_sem.at[0],
        recv_sem=hist_sem.at[1],
        device_id=later,
        device_id_type=MESH,
    )
    history.start()

    def sib_copy(w):
        return pltpu.make_async_remote_copy(
            src_ref=w2.at[:, pl.ds(w * TD, TD)],
            dst_ref=w2.at[:, pl.ds(seg_cols + w * TD, TD)],
            send_sem=sib_ss.at[w],
            recv_sem=sib_rs.at[w],
            device_id=sibling,
            device_id_type=MESH,
        )

    shape = (2 * ZN * per_dest, VS)
    row = lax.broadcasted_iota(jnp.int32, shape, 0)
    lane = lax.broadcasted_iota(jnp.int32, shape, 1)
    stage_of = row // per_stage
    up = (row // per_dest) % 2
    dest = jnp.where(up == 0, z + ZN - 1 - stage_of, z + 1 + stage_of) % ZN
    vrow = ((dest * 2 + up) * 2 + c) * per_dest + row % per_dest
    mine = jnp.where(lane == vrow, src_ref[...].astype(F32), 0.0)
    channel = jnp.sum(mine, axis=1, keepdims=True).astype(jnp.int32) - g * rows
    alive = 1.0 - dead_ref[...].astype(F32)
    here = lax.broadcasted_iota(jnp.int32, (shape[0], rows), 1) == channel
    onehot = jnp.where(here, alive, 0.0).astype(BF16)

    def pick(m):
        picked[m] = jnp.dot(
            onehot, w2[:, m * TD : (m + 1) * TD], preferred_element_type=F32
        ).astype(BF16)

    half_raw = win_raw // 2
    raw_copies[NWIN - 1].wait()
    for w in reversed(range(NWIN)):
        if w > 0:
            raw_copies[w - 1].wait()
        else:
            history.wait()
            raw[:, 0:TAPS] = jnp.where(t > 0, raw[:, 0:TAPS], jnp.zeros((rows, TAPS), BF16))
        dec = []
        for j in range(2):
            first = w * win_raw + j * half_raw
            dec.append(
                lax.dot_general(
                    raw[:, first : first + TAPS + half_raw], fir_ref[...], NT,
                    preferred_element_type=F32,
                ).astype(BF16)
            )
        spectrum = jnp.dot(
            jnp.concatenate(dec, axis=1), table_ref[...], preferred_element_type=F32
        )
        real, imag = spectrum[:, :HALF], spectrum[:, HALF:]
        amplitude = jnp.sqrt(real * real + imag * imag)
        high = amplitude.astype(BF16)
        rest = amplitude - high.astype(F32)
        middle = rest.astype(BF16)
        low = (rest - middle.astype(F32)).astype(BF16)
        level = jnp.dot(high, band_ref[...], preferred_element_type=F32)
        level += jnp.dot(middle, band_ref[...], preferred_element_type=F32)
        level += jnp.dot(low, band_ref[...], preferred_element_type=F32)
        factor = 1.0 / (level / (2 * HW + 1) + 1e-06)
        w2[:, w * TD : w * TD + HALF] = (real * factor).astype(BF16)
        w2[:, w * TD + HALF : (w + 1) * TD] = (imag * factor).astype(BF16)
        sib_copy(w).start()
    for w in reversed(range(NWIN)):
        pick(w)
    for w in reversed(range(NWIN)):
        sib_copy(w).wait_recv()
        pick(NWIN + w)

    def span(s):
        return pl.ds(pl.multiple_of(s * per_stage, per_stage), per_stage)

    def rs_copy(s, r):
        return pltpu.make_async_remote_copy(
            src_ref=picked.at[(g + r) % GN, span(s)],
            dst_ref=landed.at[s, r - 1],
            send_sem=rs_ss.at[s, r - 1],
            recv_sem=rs_rs.at[s, r - 1],
            device_id=member(r),
            device_id_type=MESH,
        )

    def ag_copy(s, r, owner):
        return pltpu.make_async_remote_copy(
            src_ref=gath.at[owner, span(s)],
            dst_ref=gath.at[owner, span(s)],
            send_sem=ag_ss.at[s, r - 1],
            recv_sem=ag_rs.at[s, r - 1],
            device_id=member(r),
            device_id_type=MESH,
        )

    def send_picked(s):
        for r in range(1, GN):
            rs_copy(s, r).start()

    def combine(s):
        for r in range(1, GN):
            rs_copy(s, r).wait_recv()
        total = picked[g, span(s)].astype(F32)
        for r in range(1, GN):
            total += landed[s, r - 1].astype(F32)
        gath[g, span(s)] = total.astype(BF16)
        for r in range(1, GN):
            ag_copy(s, r, g).start()

    def rotate(s):
        cos = [lag_ref[m : m + 1, :HALF] for m in range(5)]
        sin = [lag_ref[m : m + 1, HALF:] for m in range(5)]
        for m in range(GN):
            for h in range(2):
                first = pl.multiple_of(s * per_stage + h * per_dest, per_dest)
                a = gath[m, pl.ds(first, per_dest), :HALF].astype(F32)
                b = gath[m, pl.ds(first, per_dest), HALF:].astype(F32)

                def put(lag, real, imag):
                    at = (h * NLAG + lag) * per_dest
                    lagged[at : at + per_dest, m * TD : m * TD + HALF] = real.astype(BF16)
                    lagged[at : at + per_dest, m * TD + HALF : (m + 1) * TD] = imag.astype(BF16)

                mid = NLAG // 2
                put(mid, a * cos[0], b * cos[0])
                for n in range(1, mid + 1):
                    ac, bs, bc, as_ = a * cos[n], b * sin[n], b * cos[n], a * sin[n]
                    put(mid - n, ac - bs, bc + as_)
                    if n < mid:
                        put(mid + n, ac + bs, bc - as_)

    def ring_copy(s, h, u):
        where = (h, s, pl.ds(u * sub_rows, sub_rows))
        return pltpu.make_async_remote_copy(
            src_ref=going.at[where],
            dst_ref=coming.at[where],
            send_sem=ring_ss.at[h, s, u],
            recv_sem=ring_rs.at[h, s, u],
            device_id=above if h == 0 else below,
            device_id_type=MESH,
        )

    def x_copy(u):
        return pltpu.make_async_remote_copy(
            src_ref=xgoing.at[pl.ds(u * sub_rows, sub_rows)],
            dst_ref=xcoming.at[pl.ds(u * sub_rows, sub_rows)],
            send_sem=x_ss.at[u],
            recv_sem=x_rs.at[u],
            device_id=across,
            device_id_type=MESH,
        )

    lanes = NLAG * per_dest
    for s in range(LEAD_RS):
        send_picked(s)
    for s in range(LEAD_AG):
        combine(s)

    def stage(s, carry):
        @pl.when(s + LEAD_AG < ZN)
        def _():
            combine(s + LEAD_AG)

        @pl.when(s + LEAD_RS < ZN)
        def _():
            send_picked(s + LEAD_RS)

        for r in range(1, GN):
            ag_copy(s, r, (g + GN - r) % GN).wait_recv()
        rotate(s)
        for u in range(SUBS):
            at = slice(u * sub_rows, (u + 1) * sub_rows)
            part[at] = lax.dot_general(
                w2[at], lagged[...], NT, preferred_element_type=F32
            )

            @pl.when(s > 0)
            def _():
                for h in range(2):
                    ring_copy(s - 1, h, u).wait_recv()
                    cols = slice(h * lanes, (h + 1) * lanes)
                    part[at, cols] += coming[h, s - 1, at].astype(F32)

            @pl.when(s < ZN - 1)
            def _():
                for h in range(2):
                    going[h, s, at] = part[at, h * lanes : (h + 1) * lanes].astype(BF16)
                    ring_copy(s, h, u).start()

            @pl.when(s == ZN - 1)
            def _():
                low, high = part[at, :lanes], part[at, lanes:]
                kept[at] = jnp.where(xh == 0, low, high)
                xgoing[at] = jnp.where(xh == 0, high, low).astype(BF16)
                x_copy(u).start()

        return carry

    lax.fori_loop(0, ZN, stage, 0)

    for u in range(SUBS):
        x_copy(u).wait_recv()
    total = (kept[...] + xcoming[...].astype(F32)).T * alive
    for lag in range(NLAG):
        out_ref[:, lag, :] = total[lag * per_dest : (lag + 1) * per_dest]

    for w in range(NWIN):
        sib_copy(w).wait_send()

    def drain(s, carry):
        for r in range(1, GN):
            rs_copy(s, r).wait_send()
            ag_copy(s, r, g).wait_send()
        return carry

    lax.fori_loop(0, ZN, drain, 0)

    def drain_ring(s, carry):
        for h in range(2):
            for u in range(SUBS):
                ring_copy(s, h, u).wait_send()
        return carry

    lax.fori_loop(0, ZN - 1, drain_ring, 0)
    for u in range(SUBS):
        x_copy(u).wait_send()


def local(raw_traces, fir_taps, sources, dead_flags):
    rows, samples = raw_traces.shape
    tn = lax.axis_size("tm")
    gain = 1.0 / math.sqrt(tn * NWIN * TD)
    per_stage = VS // (2 * ZN)
    per_dest = per_stage // 2
    cols = 2 * NWIN * TD
    vmem = pl.BlockSpec(memory_space=pltpu.VMEM)
    dma = pltpu.SemaphoreType.DMA
    return pl.pallas_call(
        kernel,
        name="correlate",
        out_shape=jax.ShapeDtypeStruct((per_dest, NLAG, rows), F32),
        in_specs=[pl.BlockSpec(memory_space=pl.ANY)] + [vmem] * 6,
        out_specs=vmem,
        scratch_shapes=[
            pltpu.VMEM((rows, TAPS + samples), BF16),
            pltpu.VMEM((rows, cols), BF16),
            pltpu.VMEM((GN, VS // 2, TD), BF16),
            pltpu.VMEM((ZN, GN - 1, per_stage, TD), BF16),
            pltpu.VMEM((GN, VS // 2, TD), BF16),
            pltpu.VMEM((2 * NLAG * per_dest, cols), BF16),
            pltpu.VMEM((rows, 2 * NLAG * per_dest), F32),
            pltpu.VMEM((2, ZN - 1, rows, NLAG * per_dest), BF16),
            pltpu.VMEM((2, ZN - 1, rows, NLAG * per_dest), BF16),
            pltpu.VMEM((rows, NLAG * per_dest), F32),
            pltpu.VMEM((rows, NLAG * per_dest), BF16),
            pltpu.VMEM((rows, NLAG * per_dest), BF16),
            dma((NWIN,)),
            dma((2,)),
            dma((NWIN,)),
            dma((NWIN,)),
            dma((ZN, GN - 1)),
            dma((ZN, GN - 1)),
            dma((ZN, GN - 1)),
            dma((ZN, GN - 1)),
            dma((2, ZN - 1, SUBS)),
            dma((2, ZN - 1, SUBS)),
            dma((SUBS,)),
            dma((SUBS,)),
        ],
        compiler_params=pltpu.CompilerParams(
            collective_id=0, has_side_effects=True, vmem_limit_bytes=56 * 1024 * 1024
        ),
    )(
        raw_traces,
        fir_rows(fir_taps, HALF),
        dft_table(),
        band_matrix(),
        lag_tables(gain),
        sources[None, :],
        dead_flags[None, :],
    )


def solution(mesh):
    return jax.shard_map(
        local,
        mesh=mesh,
        in_specs=(P("chan", "tm"), P(), P(), P("chan")),
        out_specs=P("tm", None, "chan"),
        check_vma=False,
    )
```

time: 300 us -> 75.5 us (0.25)
  waiting for transfers between devices: 219 us -> 0 us
  Pallas kernels: 0 us -> 70.4 us
  local copies, waits for them, and re-layouts: 28.8 us -> 4.19 us
  other arithmetic: 18.9 us -> 0.73 us
  matrix products: 16.5 us -> 0 us
  between operations: 13.6 us -> 0.02 us
    reduce_scatter x1 -> x0, waiting for transfers between devices: 133 us -> none  [local(): lax.psum_scatter(lax.dot_general(lagged, white_flat, (((1,), (1,)), ((),...]
    psum x1 -> x0, waiting for transfers between devices: 85.8 us -> none  [local(): source = lax.psum(picked.astype(jnp.bfloat16), 'chan')]
    pallas_call x0 -> x1, Pallas kernels: none -> 70.4 us  [local(): pl.pallas_call(kernel, name='correlate', out_shape=jax.ShapeDtypeStruct((...]
    dot_general x5 -> x0, matrix products: 16.5 us -> none  [the longest x1 11.5 us: local(): lax.dot_general(lagged, white_flat, (((1,), (1,)), ((), ())), preferred_e...]
    unnamed x6 -> x1, local copies, waits for them, and re-layouts: 15.5 us -> 1.72 us
    concatenate x1 -> x0, local copies, waits for them, and re-layouts: 8.92 us -> none  [local(): jnp.concatenate([before, grouped], axis=2).reshape(-1, TAPS + sample_block)]
    unnamed x2 -> x0, other arithmetic: 6.63 us -> none
    another operation x2 -> x0, other arithmetic: 6.01 us -> none
  transfers between devices with their start and end apart: 3 -> 0, of which waited for: 2 -> 0; matrix products, arithmetic and copies ran while one was open for 6% -> 0% of each run, Pallas kernels for 0% -> 0%
where the time goes in v1:
time: 75.5 us; the launch traced here: 75.4 us
  Pallas kernels  70.4 us (93%)
  local copies, waits for them, and re-layouts  4.19 us (6%)
    pallas_call x1, Pallas kernels, local(): pl.pallas_call(kernel, name='correlate', out_shape=jax.ShapeDtypeStruct((...  70.4 us
    unnamed x1, local copies, waits for them, and re-layouts  1.72 us

profile of v1, /device:TPU:2, one launch (start us, length us, event | category | flops | bytes accessed | tf_op | source)
XLA Modules:
  0.0 75.4 jit_solution(4124690553960322473)
XLA Ops:
  0.0 0.7 pad_maximum_fusion
  0.7 1.3 %broadcast_in_dim.11.dead_ref = s32[1,640]{1,0:T(1,128)} reshape(s32[640]{0:T(1024)} %param.10) | data formatting | bytes 5120 | tf_op jit(solution)/shard_map/broadcast_in_dim | solution.py:385
  2.0 0.4 tile.10
  2.4 0.8 %reshape.4.fir_ref = bf16[128,640]{1,0:T(8,128)(2,1)} reshape(bf16[81920]{0:T(1024)(128)(2,1)S(1)} %slice.4) | data formatting | bytes 327680 | tf_op jit(solution)/shard_map/reshape | solution.py:37
  3.2 70.4 %correlate.1 = f32[16,8,640]{2,1,0:T(8,128)} custom-call(bf16[640,4096]{1,0:T(8,128)(2,1)} %raw_ref.1, bf16[128,640]{1,0:T(8,128)(2,1)} %reshape.4.fir_ref, bf16[256,256]{1,0:T(8,128)(2,1)} %constant.10.clone.table_ref, bf16[128,128]{1,0:T(8,128)(2,1)} %constant.11.clone.band_ref, f32[8,256]{1,0:T(8,128)} %constant.12.clone.lag_ref, s32[1,512]{1,0:T(1,128)} %bitcast.1, ...), custom_call_target="tpu_custom_call" | custom-call | tf_op jit(solution)/shard_map/correlate/pallas_call | solution.py:343
  73.6 1.7 %copy.9 = f32[16,8,640]{2,1,0:T(8,128)} copy(f32[16,8,640]{2,1,0:T(8,128)} %correlate.1) | data formatting | bytes 655360
  (3 shorter events, 0.0 us)

commit v2 on v1

v2 whole, which is shorter than its diff:
```python
import functools
import math

import jax
import jax.numpy as jnp
import numpy as np
from jax import lax
from jax.experimental import pallas as pl
from jax.experimental.pallas import tpu as pltpu
from jax.sharding import PartitionSpec as P

VS = 512
TD = 256
NWIN = 4
NLAG = 8
HW = 32
TAPS = 128
DECIM = 4
HALF = TD // 2
MESH = pl.DeviceIdType.MESH
F32 = jnp.float32
BF16 = jnp.bfloat16
NT = (((1,), (1,)), ((), ()))

ZN = 8
GN = 8
SUBS = 2
EARLY = 2
AHEAD = 3
HOPS = 7
VMEM_LIMIT = 63 * 1024 * 1024


def dft_table():
    phase = np.arange(TD)[:, None] * np.arange(HALF)[None, :] % TD
    angles = np.float32(2.0 * math.pi / TD) * phase.astype(np.float32)
    return jnp.asarray(np.concatenate([np.cos(angles), -np.sin(angles)], axis=1), dtype=BF16)


def lag_tables(gain):
    phase = np.arange(NLAG)[:, None] * np.arange(HALF)[None, :] % TD
    angles = np.float32(2.0 * math.pi / TD) * phase.astype(np.float32)
    both = np.concatenate([np.cos(angles), np.sin(angles)], axis=1)
    return jnp.asarray((both * np.float32(gain)).astype(np.float32))


def band_matrix():
    bins = np.arange(HALF)
    near = np.abs(bins[:, None] - bins[None, :]) <= HW
    return jnp.asarray(np.concatenate([near, near], axis=0), dtype=BF16)


def kernel(
    raw_ref, taps_hbm, table_hbm, band_hbm, lag_hbm, src_hbm, dead_hbm, out_ref,
    taps_ref, table_ref, band_ref, lag_ref, src_ref, dead_ref, raw, w2, picked, landed, gath, lagged, part, own_go, own_come, far_go, far_come, x_go, x_come, kept,
    small_sem, raw_sem, hist_sem, sib_ss, sib_rs, rs_ss, rs_rs, ag_ss, ag_rs,
    own_ss, own_rs, far_ss, far_rs, x_ss, x_rs,
):
    rows, samples = raw_ref.shape
    win_raw = TD * DECIM
    seg_cols = NWIN * TD
    per_stage = VS // (2 * ZN)
    per_dest = per_stage // 2
    lanes = NLAG * per_dest
    sub_rows = rows // SUBS
    t, g = lax.axis_index("tm"), lax.axis_index("chan")
    tn = lax.axis_size("tm")
    z, xh, c = t // 4, (t // 2) % 2, t % 2
    own = (xh + c) % 2
    own_z = (z + ZN + 1 - 2 * own) % ZN
    far_z = (z + ZN - 1 + 2 * own) % ZN
    sibling = (t + 1 - 2 * c, g)
    own_next = (own_z * 4 + xh * 2 + c, g)
    far_next = (far_z * 4 + xh * 2 + c, g)
    diagonal = (far_z * 4 + (1 - xh) * 2 + c, g)
    diagonal_from = (own_z * 4 + (1 - xh) * 2 + c, g)
    across = (z * 4 + (1 - xh) * 2 + c, g)
    later = ((t + 1) % tn, g)
    earlier = ((t + tn - 1) % tn, g)

    def member(r):
        return (t, (g + r) % GN)

    barrier = pltpu.get_barrier_semaphore()
    peers = [sibling, own_next, far_next, diagonal, diagonal_from, across, later, earlier]
    peers += [member(r) for r in range(1, GN)]
    for peer in peers:
        pl.semaphore_signal(barrier, inc=1, device_id=peer, device_id_type=MESH)

    raw_copies = [
        pltpu.make_async_copy(
            raw_ref.at[:, pl.ds(w * win_raw, win_raw)],
            raw.at[:, pl.ds(TAPS + w * win_raw, win_raw)],
            raw_sem.at[w],
        )
        for w in range(NWIN)
    ]
    small_copies = [
        pltpu.make_async_copy(here, there, small_sem.at[i])
        for i, (here, there) in enumerate(
            [
                (taps_hbm, taps_ref), (src_hbm, src_ref), (dead_hbm, dead_ref),
                (table_hbm, table_ref), (band_hbm, band_ref), (lag_hbm, lag_ref),
            ]
        )
    ]
    for copy in small_copies:
        copy.start()
    for w in reversed(range(NWIN)):
        raw_copies[w].start()
    for copy in small_copies[:3]:
        copy.wait()

    half_raw = win_raw // 2
    width = TAPS + half_raw
    fir = jnp.concatenate(
        [
            jnp.broadcast_to(taps_ref[...].astype(F32), (HALF, TAPS)),
            jnp.zeros((HALF, half_raw), F32),
        ],
        axis=1,
    )
    fir = pltpu.roll(fir, 1, 1)
    out_row = lax.broadcasted_iota(jnp.int32, (HALF, width), 0)
    for bit in range(7):
        fir = jnp.where((out_row >> bit) % 2 == 1, pltpu.roll(fir, DECIM << bit, 1), fir)
    fir = fir.astype(BF16)

    shape = (2 * ZN * per_dest, VS)
    row = lax.broadcasted_iota(jnp.int32, shape, 0)
    lane = lax.broadcasted_iota(jnp.int32, shape, 1)
    stage_of = row // per_stage
    ring = (row // per_dest) % 2
    dest = jnp.where(ring == 0, z + ZN - 1 - stage_of, z + 1 + stage_of) % ZN
    vrow = ((dest * 2 + (ring + c) % 2) * 2 + c) * per_dest + row % per_dest
    mine = jnp.where(lane == vrow, src_ref[...].astype(F32), 0.0)
    channel = jnp.sum(mine, axis=1, keepdims=True).astype(jnp.int32) - g * rows
    alive = 1.0 - dead_ref[...].astype(F32).reshape(1, rows)
    here = lax.broadcasted_iota(jnp.int32, (shape[0], rows), 1) == channel
    onehot = jnp.where(here, alive, 0.0).astype(BF16)

    def sib_copy(w):
        return pltpu.make_async_remote_copy(
            src_ref=w2.at[:, pl.ds(w * TD, TD)],
            dst_ref=w2.at[:, pl.ds(seg_cols + w * TD, TD)],
            send_sem=sib_ss.at[w],
            recv_sem=sib_rs.at[w],
            device_id=sibling,
            device_id_type=MESH,
        )

    def window(w):
        dec = []
        for j in range(2):
            first = w * win_raw + j * half_raw
            dec.append(
                lax.dot_general(
                    raw[:, first : first + width], fir, NT, preferred_element_type=F32
                ).astype(BF16)
            )
        spectrum = jnp.dot(
            jnp.concatenate(dec, axis=1), table_ref[...], preferred_element_type=F32
        )
        real, imag = spectrum[:, :HALF], spectrum[:, HALF:]
        amplitude = jnp.sqrt(real * real + imag * imag)
        high = amplitude.astype(BF16)
        low = (amplitude - high.astype(F32)).astype(BF16)
        level = jnp.dot(
            jnp.concatenate([high, low], axis=1), band_ref[...], preferred_element_type=F32
        )
        factor = 1.0 / (level * (1.0 / (2 * HW + 1)) + 1e-06)
        w2[:, w * TD : w * TD + HALF] = (real * factor).astype(BF16)
        w2[:, w * TD + HALF : (w + 1) * TD] = (imag * factor).astype(BF16)

    def span(s):
        return pl.ds(pl.multiple_of(s * per_stage, per_stage), per_stage)

    def rs_copy(s, r):
        return pltpu.make_async_remote_copy(
            src_ref=picked.at[(g + r) % GN, span(s)],
            dst_ref=landed.at[s, r - 1],
            send_sem=rs_ss,
            recv_sem=rs_rs.at[s],
            device_id=member(r),
            device_id_type=MESH,
        )

    def ag_copy(s, r):
        return pltpu.make_async_remote_copy(
            src_ref=gath.at[0, span(s)],
            dst_ref=gath.at[r, span(s)],
            send_sem=ag_ss,
            recv_sem=ag_rs.at[s],
            device_id=member(r),
            device_id_type=MESH,
        )

    def pick(m):
        picked[m] = jnp.dot(
            onehot, w2[:, m * TD : (m + 1) * TD], preferred_element_type=F32
        ).astype(BF16)
        r = (m + GN - g) % GN

        @pl.when(r != 0)
        def _():
            for s in range(EARLY):
                rs_copy(s, r).start()

    def send_picked(s):
        for r in range(1, GN):
            rs_copy(s, r).start()

    def combine(s):
        pltpu.make_async_copy(landed.at[s], landed.at[s], rs_rs.at[s]).wait()
        total = picked[g, span(s)].astype(F32)
        for r in range(1, GN):
            total += landed[s, r - 1].astype(F32)
        gath[0, span(s)] = total.astype(BF16)
        for r in range(1, GN):
            ag_copy(s, r).start()

    def ag_wait(s):
        there = gath.at[pl.ds(1, GN - 1), span(s)]
        pltpu.make_async_copy(there, there, ag_rs.at[s]).wait()

    def rotate(s):
        cos = [lag_ref[m : m + 1, :HALF] for m in range(5)]
        sin = [lag_ref[m : m + 1, HALF:] for m in range(5)]
        for r in range(GN):
            col = pl.multiple_of((g + GN - r) % GN * TD, TD)
            for h in range(2):
                first = pl.multiple_of(s * per_stage + h * per_dest, per_dest)
                a = gath[r, pl.ds(first, per_dest), :HALF].astype(F32)
                b = gath[r, pl.ds(first, per_dest), HALF:].astype(F32)

                def put(lag, real, imag):
                    at = (h * NLAG + lag) * per_dest
                    both = jnp.concatenate([real.astype(BF16), imag.astype(BF16)], axis=1)
                    lagged[at : at + per_dest, pl.ds(col, TD)] = both

                mid = NLAG // 2
                put(mid, a * cos[0], b * cos[0])
                for n in range(1, mid + 1):
                    ac, bs, bc, as_ = a * cos[n], b * sin[n], b * cos[n], a * sin[n]
                    put(mid - n, ac - bs, bc + as_)
                    if n < mid:
                        put(mid + n, ac + bs, bc - as_)

    def piece(u):
        return pl.ds(u * sub_rows, sub_rows)

    def own_copy(s, u):
        return pltpu.make_async_remote_copy(
            src_ref=own_go.at[s, piece(u)],
            dst_ref=own_come.at[s, piece(u)],
            send_sem=own_ss,
            recv_sem=own_rs.at[s, u],
            device_id=own_next,
            device_id_type=MESH,
        )

    def far_copy(s, u, to):
        return pltpu.make_async_remote_copy(
            src_ref=far_go.at[s, piece(u)],
            dst_ref=far_come.at[s, piece(u)],
            send_sem=far_ss,
            recv_sem=far_rs.at[s, u],
            device_id=to,
            device_id_type=MESH,
        )

    def x_copy(s, u):
        return pltpu.make_async_remote_copy(
            src_ref=x_go.at[s - HOPS, piece(u)],
            dst_ref=x_come.at[s - HOPS, piece(u)],
            send_sem=x_ss,
            recv_sem=x_rs.at[s - HOPS, u],
            device_id=across,
            device_id_type=MESH,
        )

    own_lanes = pl.ds(pl.multiple_of(own * lanes, lanes), lanes)
    far_lanes = pl.ds(pl.multiple_of((1 - own) * lanes, lanes), lanes)

    def dot(s, u):
        at = slice(u * sub_rows, (u + 1) * sub_rows)
        part[s % 2, at] = lax.dot_general(w2[at], lagged[...], NT, preferred_element_type=F32)

        @pl.when(s >= HOPS)
        def _():
            x_go[s - HOPS, at] = part[s % 2, at, far_lanes].astype(BF16)
            x_copy(s, u).start()

    def turn(s, u):
        at = slice(u * sub_rows, (u + 1) * sub_rows)

        @pl.when(s > 0)
        def _():
            own_copy(s - 1, u).wait_recv()
            part[s % 2, at, own_lanes] += own_come[s - 1, at].astype(F32)

        @pl.when(s == HOPS)
        def _():
            far_copy(HOPS - 1, u, diagonal).wait_recv()
            part[s % 2, at, own_lanes] += far_come[HOPS - 1, at].astype(F32)

        @pl.when(s >= HOPS)
        def _():
            x_copy(s, u).wait_recv()
            part[s % 2, at, own_lanes] += x_come[s - HOPS, at].astype(F32)

        @pl.when(s < ZN - 1)
        def _():
            own_go[s, at] = part[s % 2, at, own_lanes].astype(BF16)
            own_copy(s, u).start()

        @pl.when(s == ZN - 1)
        def _():
            kept[at] = part[s % 2, at, own_lanes]

        @pl.when((s > 0) & (s < HOPS))
        def _():
            far_copy(s - 1, u, far_next).wait_recv()
            part[s % 2, at, far_lanes] += far_come[s - 1, at].astype(F32)

        @pl.when(s < HOPS)
        def _():
            far_go[s, at] = part[s % 2, at, far_lanes].astype(BF16)

        @pl.when(s < HOPS - 1)
        def _():
            far_copy(s, u, far_next).start()

        @pl.when(s == HOPS - 1)
        def _():
            far_copy(s, u, diagonal).start()

    pl.semaphore_wait(barrier, len(peers))
    history = pltpu.make_async_remote_copy(
        src_ref=raw_ref.at[:, pl.ds(samples - TAPS, TAPS)],
        dst_ref=raw.at[:, pl.ds(0, TAPS)],
        send_sem=hist_sem.at[0],
        recv_sem=hist_sem.at[1],
        device_id=later,
        device_id_type=MESH,
    )
    history.start()
    for copy in small_copies[3:]:
        copy.wait()
    for w in (3, 2):
        raw_copies[w].wait()
    window(3)
    sib_copy(3).start()
    for w in (2, 1):
        raw_copies[w - 1].wait()
        window(w)
        sib_copy(w).start()
    for w in (3, 2, 1):
        pick(w)
    for w in (3, 2):
        sib_copy(w).wait_recv()
        pick(NWIN + w)
    history.wait()
    raw[:, 0:TAPS] = jnp.where(t > 0, raw[:, 0:TAPS], jnp.zeros((rows, TAPS), BF16))
    window(0)
    sib_copy(0).start()
    pick(0)
    sib_copy(1).wait_recv()
    pick(NWIN + 1)
    sib_copy(0).wait_recv()
    pick(NWIN)
    combine(0)
    send_picked(2)
    combine(1)
    send_picked(3)
    combine(2)
    first = jnp.int32(0)
    ag_wait(0)
    rotate(0)
    for u in range(SUBS):
        dot(first, u)
        turn(first, u)
    send_picked(4)
    combine(3)
    ag_wait(1)
    rotate(1)
    for u in range(SUBS):
        dot(first + 1, u)
    send_picked(5)

    def stage(s, carry):
        for u in range(SUBS):
            @pl.when((s >= AHEAD) & (s + 1 < ZN))
            def _():
                if u == 0:
                    ag_wait(s + 1)
                    rotate(s + 1)
                dot(s + 1, u)

            turn(s, u)
            if u == 0:
                @pl.when(s + 3 < ZN)
                def _():
                    combine(s + 3)

                @pl.when(s + 5 < ZN)
                def _():
                    send_picked(s + 5)

        @pl.when(s < AHEAD)
        def _():
            ag_wait(s + 1)
            rotate(s + 1)
            for u in range(SUBS):
                dot(s + 1, u)

        return carry

    lax.fori_loop(1, ZN, stage, 0)

    total = kept[...].T * alive
    for lag in range(NLAG):
        out_ref[:, lag, :] = total[lag * per_dest : (lag + 1) * per_dest]

    for w in range(NWIN):
        sib_copy(w).wait_send()
    sent = [
        (picked.at[pl.ds(0, GN - 1)], rs_ss), (gath.at[pl.ds(0, GN - 1)], ag_ss),
        (own_go, own_ss), (far_go, far_ss), (x_go, x_ss),
    ]
    for what, sem in sent:
        pltpu.make_async_copy(what, what, sem).wait()


def local(raw_traces, fir_taps, sources, dead_flags):
    rows, samples = raw_traces.shape
    tn = lax.axis_size("tm")
    gain = 1.0 / math.sqrt(tn * NWIN * TD)
    per_stage = VS // (2 * ZN)
    per_dest = per_stage // 2
    lanes = NLAG * per_dest
    cols = 2 * NWIN * TD
    hbm = pl.BlockSpec(memory_space=pltpu.HBM)
    vmem = pl.BlockSpec(memory_space=pltpu.VMEM)
    dma = pltpu.SemaphoreType.DMA
    return pl.pallas_call(
        kernel,
        name="correlate",
        out_shape=jax.ShapeDtypeStruct((per_dest, NLAG, rows), F32),
        in_specs=[hbm] * 7,
        out_specs=vmem,
        scratch_shapes=[
            pltpu.VMEM((1, TAPS), BF16),
            pltpu.VMEM((TD, TD), BF16),
            pltpu.VMEM((TD, HALF), BF16),
            pltpu.VMEM((NLAG, TD), F32),
            pltpu.VMEM((1, VS), jnp.int32),
            pltpu.VMEM((rows,), jnp.int32),
            pltpu.VMEM((rows, TAPS + samples), BF16),
            pltpu.VMEM((rows, cols), BF16),
            pltpu.VMEM((GN, VS // 2, TD), BF16),
            pltpu.VMEM((ZN, GN - 1, per_stage, TD), BF16),
            pltpu.VMEM((GN, VS // 2, TD), BF16),
            pltpu.VMEM((2 * lanes, cols), BF16),
            pltpu.VMEM((2, rows, 2 * lanes), F32),
            pltpu.VMEM((ZN - 1, rows, lanes), BF16),
            pltpu.VMEM((ZN - 1, rows, lanes), BF16),
            pltpu.VMEM((HOPS, rows, lanes), BF16),
            pltpu.VMEM((HOPS, rows, lanes), BF16),
            pltpu.VMEM((ZN - HOPS, rows, lanes), BF16),
            pltpu.VMEM((ZN - HOPS, rows, lanes), BF16),
            pltpu.VMEM((rows, lanes), F32),
            dma((6,)),
            dma((NWIN,)),
            dma((2,)),
            dma((NWIN,)),
            dma((NWIN,)),
            dma,
            dma((ZN,)),
            dma,
            dma((ZN,)),
            dma,
            dma((ZN - 1, SUBS)),
            dma,
            dma((HOPS, SUBS)),
            dma,
            dma((ZN - HOPS, SUBS)),
        ],
        compiler_params=pltpu.CompilerParams(
            collective_id=0, has_side_effects=True, vmem_limit_bytes=VMEM_LIMIT
        ),
    )(
        raw_traces,
        fir_taps[None, :],
        dft_table(),
        band_matrix(),
        lag_tables(gain),
        sources[None, :],
        dead_flags,
    )


def solution(mesh):
    return jax.shard_map(
        local,
        mesh=mesh,
        in_specs=(P("chan", "tm"), P(), P(), P("chan")),
        out_specs=P("tm", None, "chan"),
        check_vma=False,
    )
```

time: 75.5 us -> 67.2 us (0.89)
  Pallas kernels: 70.4 us -> 65.3 us
  local copies, waits for them, and re-layouts: 4.19 us -> 1.72 us
    pallas_call x1, Pallas kernels: 70.4 us -> 65.3 us  [local(): pl.pallas_call(kernel, name='correlate', out_shape=jax.ShapeDtypeStruct((...]
    broadcast_in_dim x2 -> x0, local copies, waits for them, and re-layouts: 1.28 us -> none  [the longest x1 1.28 us: local(): dead_flags[None, :]]
    reshape x1 -> x0, local copies, waits for them, and re-layouts: 0.8 us -> none  [fir_rows(): jnp.tile(padded_taps, out_block)[:out_block * width]]
where the time goes in v2:
time: 67.2 us; the launch traced here: 67.1 us
  Pallas kernels  65.3 us (97%)
  local copies, waits for them, and re-layouts  1.72 us (3%)
    pallas_call x1, Pallas kernels, local(): pl.pallas_call(kernel, name='correlate', out_shape=jax.ShapeDtypeStruct((...  65.3 us
    unnamed x1, local copies, waits for them, and re-layouts  1.72 us

profile of v2, /device:TPU:2, one launch (start us, length us, event | category | flops | bytes accessed | tf_op | source)
XLA Modules:
  0.0 67.1 jit_solution(12523945130731142844)
XLA Ops:
  0.0 65.3 %correlate.1 = f32[16,8,640]{2,1,0:T(8,128)} custom-call(bf16[640,4096]{1,0:T(8,128)(2,1)} %raw_ref.1, bf16[1,128]{1,0:T(2,128)(2,1)} %bitcast.3, bf16[256,256]{1,0:T(8,128)(2,1)} %constant.6.clone.table_hbm, bf16[256,128]{1,0:T(8,128)(2,1)} %constant.7.clone.band_hbm, f32[8,256]{1,0:T(8,128)} %constant.8.clone.lag_hbm, s32[1,512]{1,0:T(1,128)} %bitcast.2, ...), custom_call_target="tpu_custom_call" | custom-call | tf_op jit(solution)/shard_map/correlate/pallas_call | solution.py:446
  65.4 1.7 %copy.9 = f32[16,8,640]{2,1,0:T(8,128)} copy(f32[16,8,640]{2,1,0:T(8,128)} %correlate.1) | data formatting | bytes 655360

commit v3 on v2

--- a/solution.py
+++ b/solution.py
@@ -24,8 +24,12 @@
 
 ZN = 8
 GN = 8
-SUBS = 2
-EARLY = 2
+SUBS = 4
+DOTS = 2
+PAIRS = ((0, 3), (4, 7), (1, 2), (5, 6))
+OWNERS = ((0, 5), (2, 7), (1, 4), (3, 6))
+LEAD = 2
+MOST = 128
 AHEAD = 3
 HOPS = 7
 VMEM_LIMIT = 63 * 1024 * 1024
@@ -52,7 +56,7 @@
 
 def kernel(
     raw_ref, taps_hbm, table_hbm, band_hbm, lag_hbm, src_hbm, dead_hbm, out_ref,
-    taps_ref, table_ref, band_ref, lag_ref, src_ref, dead_ref, raw, w2, picked, landed, gath, lagged, part, own_go, own_come, far_go, far_come, x_go, x_come, kept,
+    taps_ref, table_ref, band_ref, lag_ref, src_ref, dead_ref, order_ref, raw, w2, picked, landed, gath, lagged, part, own_go, own_come, far_go, far_come, x_go, x_come, kept,
     small_sem, raw_sem, hist_sem, sib_ss, sib_rs, rs_ss, rs_rs, ag_ss, ag_rs,
     own_ss, own_rs, far_ss, far_rs, x_ss, x_rs,
 ):
@@ -63,6 +67,7 @@
     per_dest = per_stage // 2
     lanes = NLAG * per_dest
     sub_rows = rows // SUBS
+    per_dot = SUBS // DOTS
     t, g = lax.axis_index("tm"), lax.axis_index("chan")
     tn = lax.axis_size("tm")
     z, xh, c = t // 4, (t // 2) % 2, t % 2
@@ -126,18 +131,34 @@
         fir = jnp.where((out_row >> bit) % 2 == 1, pltpu.roll(fir, DECIM << bit, 1), fir)
     fir = fir.astype(BF16)
 
-    shape = (2 * ZN * per_dest, VS)
-    row = lax.broadcasted_iota(jnp.int32, shape, 0)
-    lane = lax.broadcasted_iota(jnp.int32, shape, 1)
+    many = 2 * ZN * per_dest
+    row = lax.broadcasted_iota(jnp.int32, (many, VS), 0)
+    lane = lax.broadcasted_iota(jnp.int32, (many, VS), 1)
     stage_of = row // per_stage
     ring = (row // per_dest) % 2
     dest = jnp.where(ring == 0, z + ZN - 1 - stage_of, z + 1 + stage_of) % ZN
     vrow = ((dest * 2 + (ring + c) % 2) * 2 + c) * per_dest + row % per_dest
     mine = jnp.where(lane == vrow, src_ref[...].astype(F32), 0.0)
-    channel = jnp.sum(mine, axis=1, keepdims=True).astype(jnp.int32) - g * rows
+    src_col = jnp.sum(mine, axis=1, keepdims=True)
+    row, lane = row[:, :many], lane[:, :many]
+    src_row = jnp.sum(jnp.where(row == lane, src_col, 0.0), axis=0, keepdims=True)
+    group_col = jnp.floor((src_col + 0.5) * (1.0 / rows))
+    group_row = jnp.floor((src_row + 0.5) * (1.0 / rows))
+    same = jnp.where(group_col == group_row, 1.0, 0.0)
+    rank_col = jnp.sum(jnp.where(lane < row, same, 0.0), axis=1, keepdims=True)
+    rank_row = jnp.sum(jnp.where(row < lane, same, 0.0), axis=0, keepdims=True)
+    me = g.astype(F32)
+    slot = lax.broadcasted_iota(jnp.int32, (MOST, many), 0).astype(F32)
+    filled = (slot == rank_row) & (group_row == me)
+    channel = jnp.sum(jnp.where(filled, src_row - me * rows + 1.0, 0.0), axis=1, keepdims=True)
     alive = 1.0 - dead_ref[...].astype(F32).reshape(1, rows)
-    here = lax.broadcasted_iota(jnp.int32, (shape[0], rows), 1) == channel
+    here = lax.broadcasted_iota(jnp.int32, (MOST, rows), 1) + 1 == channel.astype(jnp.int32)
     onehot = jnp.where(here, alive, 0.0).astype(BF16)
+    back = jnp.where(group_col > me, me - group_col + GN, me - group_col)
+    place = (back * MOST + rank_col).astype(jnp.int32)
+    order_ref[...] = jnp.where(
+        lax.broadcasted_iota(jnp.int32, (many, GN * MOST), 1) == place, 1.0, 0.0
+    ).astype(BF16)
 
     def sib_copy(w):
         return pltpu.make_async_remote_copy(
@@ -175,13 +196,13 @@
     def span(s):
         return pl.ds(pl.multiple_of(s * per_stage, per_stage), per_stage)
 
-    def rs_copy(s, r):
+    def rs_copy(m, p, where, owner, r):
         return pltpu.make_async_remote_copy(
-            src_ref=picked.at[(g + r) % GN, span(s)],
-            dst_ref=landed.at[s, r - 1],
+            src_ref=picked.at[m, p],
+            dst_ref=landed.at[r, :, pl.ds(where * HALF, HALF)],
             send_sem=rs_ss,
-            recv_sem=rs_rs.at[s],
-            device_id=member(r),
+            recv_sem=rs_rs,
+            device_id=(t, owner),
             device_id_type=MESH,
         )
 
@@ -189,35 +210,45 @@
         return pltpu.make_async_remote_copy(
             src_ref=gath.at[0, span(s)],
             dst_ref=gath.at[r, span(s)],
-            send_sem=ag_ss,
+            send_sem=ag_ss.at[s],
             recv_sem=ag_rs.at[s],
             device_id=member(r),
             device_id_type=MESH,
         )
 
     def pick(m):
-        picked[m] = jnp.dot(
+        value = jnp.dot(
             onehot, w2[:, m * TD : (m + 1) * TD], preferred_element_type=F32
         ).astype(BF16)
-        r = (m + GN - g) % GN
-
-        @pl.when(r != 0)
-        def _():
-            for s in range(EARLY):
-                rs_copy(s, r).start()
-
-    def send_picked(s):
-        for r in range(1, GN):
-            rs_copy(s, r).start()
-
-    def combine(s):
-        pltpu.make_async_copy(landed.at[s], landed.at[s], rs_rs.at[s]).wait()
-        total = picked[g, span(s)].astype(F32)
-        for r in range(1, GN):
-            total += landed[s, r - 1].astype(F32)
-        gath[0, span(s)] = total.astype(BF16)
+        q = [m in pair for pair in PAIRS].index(True)
+        where = PAIRS[q].index(m)
+        for p in range(2):
+            half = value[:, p * HALF : (p + 1) * HALF]
+            picked[m, p] = half
+            r = (OWNERS[q][p] + GN - g) % GN
+
+            @pl.when(r != 0)
+            def _():
+                rs_copy(m, p, where, OWNERS[q][p], r).start()
+
+            @pl.when(r == 0)
+            def _():
+                landed[0, :, where * HALF : (where + 1) * HALF] = half
+
+    def combine():
+        there = landed.at[pl.ds(1, GN - 1)]
+        pltpu.make_async_copy(there, there, rs_rs).wait()
+        gath[0] = jnp.dot(
+            order_ref[...], landed[...].reshape(GN * MOST, TD), preferred_element_type=F32
+        ).astype(BF16)
+
+    def share(s):
         for r in range(1, GN):
             ag_copy(s, r).start()
+
+    def shared(s):
+        sent = gath.at[pl.ds(0, GN - 1), span(s)]
+        pltpu.make_async_copy(sent, sent, ag_ss.at[s]).wait()
 
     def ag_wait(s):
         there = gath.at[pl.ds(1, GN - 1), span(s)]
@@ -226,17 +257,19 @@
     def rotate(s):
         cos = [lag_ref[m : m + 1, :HALF] for m in range(5)]
         sin = [lag_ref[m : m + 1, HALF:] for m in range(5)]
-        for r in range(GN):
-            col = pl.multiple_of((g + GN - r) % GN * TD, TD)
+        for m in range(GN):
+            q = [m in pair for pair in PAIRS].index(True)
+            off = PAIRS[q].index(m) * HALF
+            re_at, im_at = [(g + GN - owner) % GN for owner in OWNERS[q]]
             for h in range(2):
                 first = pl.multiple_of(s * per_stage + h * per_dest, per_dest)
-                a = gath[r, pl.ds(first, per_dest), :HALF].astype(F32)
-                b = gath[r, pl.ds(first, per_dest), HALF:].astype(F32)
+                a = gath[re_at, pl.ds(first, per_dest), off : off + HALF].astype(F32)
+                b = gath[im_at, pl.ds(first, per_dest), off : off + HALF].astype(F32)
 
                 def put(lag, real, imag):
                     at = (h * NLAG + lag) * per_dest
                     both = jnp.concatenate([real.astype(BF16), imag.astype(BF16)], axis=1)
-                    lagged[at : at + per_dest, pl.ds(col, TD)] = both
+                    lagged[at : at + per_dest, m * TD : (m + 1) * TD] = both
 
                 mid = NLAG // 2
                 put(mid, a * cos[0], b * cos[0])
@@ -282,14 +315,15 @@
     own_lanes = pl.ds(pl.multiple_of(own * lanes, lanes), lanes)
     far_lanes = pl.ds(pl.multiple_of((1 - own) * lanes, lanes), lanes)
 
-    def dot(s, u):
-        at = slice(u * sub_rows, (u + 1) * sub_rows)
+    def dot(s, d):
+        at = slice(d * per_dot * sub_rows, (d + 1) * per_dot * sub_rows)
         part[s % 2, at] = lax.dot_general(w2[at], lagged[...], NT, preferred_element_type=F32)
 
         @pl.when(s >= HOPS)
         def _():
             x_go[s - HOPS, at] = part[s % 2, at, far_lanes].astype(BF16)
-            x_copy(s, u).start()
+            for u in range(d * per_dot, (d + 1) * per_dot):
+                x_copy(s, u).start()
 
     def turn(s, u):
         at = slice(u * sub_rows, (u + 1) * sub_rows)
@@ -369,50 +403,51 @@
     pick(NWIN + 1)
     sib_copy(0).wait_recv()
     pick(NWIN)
-    combine(0)
-    send_picked(2)
-    combine(1)
-    send_picked(3)
-    combine(2)
+    combine()
+    for s in range(LEAD):
+        share(s)
+        shared(s)
+    share(LEAD)
     first = jnp.int32(0)
     ag_wait(0)
     rotate(0)
-    for u in range(SUBS):
-        dot(first, u)
-        turn(first, u)
-    send_picked(4)
-    combine(3)
+    for d in range(DOTS):
+        dot(first, d)
+        for u in range(d * per_dot, (d + 1) * per_dot):
+            turn(first, u)
+    shared(LEAD)
+    share(LEAD + 1)
     ag_wait(1)
     rotate(1)
-    for u in range(SUBS):
-        dot(first + 1, u)
-    send_picked(5)
+    for d in range(DOTS):
+        dot(first + 1, d)
 
     def stage(s, carry):
-        for u in range(SUBS):
+        @pl.when(s + LEAD < ZN)
+        def _():
+            shared(s + LEAD)
+
+        @pl.when(s + LEAD + 1 < ZN)
+        def _():
+            share(s + LEAD + 1)
+
+        for d in range(DOTS):
             @pl.when((s >= AHEAD) & (s + 1 < ZN))
             def _():
-                if u == 0:
+                if d == 0:
                     ag_wait(s + 1)
                     rotate(s + 1)
-                dot(s + 1, u)
-
-            turn(s, u)
-            if u == 0:
-                @pl.when(s + 3 < ZN)
-                def _():
-                    combine(s + 3)
-
-                @pl.when(s + 5 < ZN)
-                def _():
-                    send_picked(s + 5)
+                dot(s + 1, d)
+
+            for u in range(d * per_dot, (d + 1) * per_dot):
+                turn(s, u)
 
         @pl.when(s < AHEAD)
         def _():
             ag_wait(s + 1)
             rotate(s + 1)
-            for u in range(SUBS):
-                dot(s + 1, u)
+            for d in range(DOTS):
+                dot(s + 1, d)
 
         return carry
 
@@ -425,7 +460,7 @@
     for w in range(NWIN):
         sib_copy(w).wait_send()
     sent = [
-        (picked.at[pl.ds(0, GN - 1)], rs_ss), (gath.at[pl.ds(0, GN - 1)], ag_ss),
+        (landed.at[pl.ds(1, GN - 1)], rs_ss),
         (own_go, own_ss), (far_go, far_ss), (x_go, x_ss),
     ]
     for what, sem in sent:
@@ -456,10 +491,11 @@
             pltpu.VMEM((NLAG, TD), F32),
             pltpu.VMEM((1, VS), jnp.int32),
             pltpu.VMEM((rows,), jnp.int32),
+            pltpu.VMEM((VS // 2, GN * MOST), BF16),
             pltpu.VMEM((rows, TAPS + samples), BF16),
             pltpu.VMEM((rows, cols), BF16),
-            pltpu.VMEM((GN, VS // 2, TD), BF16),
-            pltpu.VMEM((ZN, GN - 1, per_stage, TD), BF16),
+            pltpu.VMEM((GN, 2, MOST, HALF), BF16),
+            pltpu.VMEM((GN, MOST, TD), BF16),
             pltpu.VMEM((GN, VS // 2, TD), BF16),
             pltpu.VMEM((2 * lanes, cols), BF16),
             pltpu.VMEM((2, rows, 2 * lanes), F32),
@@ -476,8 +512,8 @@
             dma((NWIN,)),
             dma((NWIN,)),
             dma,
+            dma,
             dma((ZN,)),
-            dma,
             dma((ZN,)),
             dma,
             dma((ZN - 1, SUBS)),

time: 67.2 us -> 61.6 us (0.917)
  Pallas kernels: 65.3 us -> 59.8 us
    pallas_call x1, Pallas kernels: 65.3 us -> 59.8 us  [local(): pl.pallas_call(kernel, name='correlate', out_shape=jax.ShapeDtypeStruct((...]
where the time goes in v3:
time: 61.6 us; the launch traced here: 61.5 us
  Pallas kernels  59.8 us (97%)
  local copies, waits for them, and re-layouts  1.72 us (3%)
    pallas_call x1, Pallas kernels, local(): pl.pallas_call(kernel, name='correlate', out_shape=jax.ShapeDtypeStruct((...  59.8 us
    unnamed x1, local copies, waits for them, and re-layouts  1.72 us

profile of v3, /device:TPU:2, one launch (start us, length us, event | category | flops | bytes accessed | tf_op | source)
XLA Modules:
  0.0 61.5 jit_solution(12515262745916366970)
XLA Ops:
  0.0 59.8 %correlate.1 = f32[16,8,640]{2,1,0:T(8,128)} custom-call(bf16[640,4096]{1,0:T(8,128)(2,1)} %raw_ref.1, bf16[1,128]{1,0:T(2,128)(2,1)} %bitcast.3, bf16[256,256]{1,0:T(8,128)(2,1)} %constant.6.clone.table_hbm, bf16[256,128]{1,0:T(8,128)(2,1)} %constant.7.clone.band_hbm, f32[8,256]{1,0:T(8,128)} %constant.8.clone.lag_hbm, s32[1,512]{1,0:T(1,128)} %bitcast.2, ...), custom_call_target="tpu_custom_call" | custom-call | tf_op jit(solution)/shard_map/correlate/pallas_call | solution.py:481
  59.8 1.7 %copy.9 = f32[16,8,640]{2,1,0:T(8,128)} copy(f32[16,8,640]{2,1,0:T(8,128)} %correlate.1) | data formatting | bytes 655360

commit v4 on v3

--- a/solution.py
+++ b/solution.py
@@ -30,7 +30,6 @@
 OWNERS = ((0, 5), (2, 7), (1, 4), (3, 6))
 LEAD = 2
 MOST = 128
-AHEAD = 3
 HOPS = 7
 VMEM_LIMIT = 63 * 1024 * 1024
 
@@ -154,12 +153,6 @@
     alive = 1.0 - dead_ref[...].astype(F32).reshape(1, rows)
     here = lax.broadcasted_iota(jnp.int32, (MOST, rows), 1) + 1 == channel.astype(jnp.int32)
     onehot = jnp.where(here, alive, 0.0).astype(BF16)
-    back = jnp.where(group_col > me, me - group_col + GN, me - group_col)
-    place = (back * MOST + rank_col).astype(jnp.int32)
-    order_ref[...] = jnp.where(
-        lax.broadcasted_iota(jnp.int32, (many, GN * MOST), 1) == place, 1.0, 0.0
-    ).astype(BF16)
-
     def sib_copy(w):
         return pltpu.make_async_remote_copy(
             src_ref=w2.at[:, pl.ds(w * TD, TD)],
@@ -403,55 +396,42 @@
     pick(NWIN + 1)
     sib_copy(0).wait_recv()
     pick(NWIN)
+    back = jnp.where(group_col > me, me - group_col + GN, me - group_col)
+    place = (back * MOST + rank_col).astype(jnp.int32)
+    order_ref[...] = jnp.where(
+        lax.broadcasted_iota(jnp.int32, (many, GN * MOST), 1) == place, 1.0, 0.0
+    ).astype(BF16)
     combine()
     for s in range(LEAD):
         share(s)
         shared(s)
     share(LEAD)
-    first = jnp.int32(0)
-    ag_wait(0)
-    rotate(0)
-    for d in range(DOTS):
-        dot(first, d)
-        for u in range(d * per_dot, (d + 1) * per_dot):
-            turn(first, u)
-    shared(LEAD)
-    share(LEAD + 1)
-    ag_wait(1)
-    rotate(1)
-    for d in range(DOTS):
-        dot(first + 1, d)
 
     def stage(s, carry):
-        @pl.when(s + LEAD < ZN)
+        @pl.when((s >= 0) & (s + LEAD < ZN))
         def _():
             shared(s + LEAD)
 
-        @pl.when(s + LEAD + 1 < ZN)
+        @pl.when((s >= 0) & (s + LEAD + 1 < ZN))
         def _():
             share(s + LEAD + 1)
 
         for d in range(DOTS):
-            @pl.when((s >= AHEAD) & (s + 1 < ZN))
+            @pl.when(s + 1 < ZN)
             def _():
                 if d == 0:
                     ag_wait(s + 1)
                     rotate(s + 1)
                 dot(s + 1, d)
 
-            for u in range(d * per_dot, (d + 1) * per_dot):
-                turn(s, u)
-
-        @pl.when(s < AHEAD)
-        def _():
-            ag_wait(s + 1)
-            rotate(s + 1)
-            for d in range(DOTS):
-                dot(s + 1, d)
+            @pl.when(s != 0)
+            def _():
+                for u in range(d * per_dot, (d + 1) * per_dot):
+                    turn(jnp.maximum(s, 0), u)
 
         return carry
 
-    lax.fori_loop(1, ZN, stage, 0)
+    lax.fori_loop(-1, ZN, stage, 0)
 
     total = kept[...].T * alive
     for lag in range(NLAG):

time: 61.6 us -> 61 us (level)
  Pallas kernels: 59.8 us -> 58.7 us
    pallas_call x1, Pallas kernels: 59.8 us -> 58.7 us  [local(): pl.pallas_call(kernel, name='correlate', out_shape=jax.ShapeDtypeStruct((...]
where the time goes in v4:
time: 61 us; the launch traced here: 60.4 us
  Pallas kernels  58.7 us (96%)
  local copies, waits for them, and re-layouts  1.72 us (3%)
    pallas_call x1, Pallas kernels, local(): pl.pallas_call(kernel, name='correlate', out_shape=jax.ShapeDtypeStruct((...  58.7 us
    unnamed x1, local copies, waits for them, and re-layouts  1.72 us

profile of v4, /device:TPU:2, one launch (start us, length us, event | category | flops | bytes accessed | tf_op | source)
XLA Modules:
  0.0 60.4 jit_solution(6236573681976653569)
XLA Ops:
  0.0 58.7 %correlate.1 = f32[16,8,640]{2,1,0:T(8,128)} custom-call(bf16[640,4096]{1,0:T(8,128)(2,1)} %raw_ref.1, bf16[1,128]{1,0:T(2,128)(2,1)} %bitcast.3, bf16[256,256]{1,0:T(8,128)(2,1)} %constant.6.clone.table_hbm, bf16[256,128]{1,0:T(8,128)(2,1)} %constant.7.clone.band_hbm, f32[8,256]{1,0:T(8,128)} %constant.8.clone.lag_hbm, s32[1,512]{1,0:T(1,128)} %bitcast.2, ...), custom_call_target="tpu_custom_call" | custom-call | tf_op jit(solution)/shard_map/correlate/pallas_call | solution.py:461
  58.7 1.7 %copy.9 = f32[16,8,640]{2,1,0:T(8,128)} copy(f32[16,8,640]{2,1,0:T(8,128)} %correlate.1) | data formatting | bytes 655360
